TPU v7x, 32 devices: a whole 2x2x4 slice. The times are simulated.
32 devices in a mesh: pts: 8 (over y, x, core), out: 4 (over z).
Axes of the slice: x: 2, y: 2, z: 4, core: 2. Of those that a mesh axis runs over, the one named last changes fastest.
Arguments:
- points: bfloat16 [32768, 1024], P('pts'), may hold values from -6 to 6
- coefficients: float32 [32768, 1024], P('pts', 'out'), may hold values from -4 to 4
- residual: float32 [32768, 1024], P('pts', 'out'), may hold values from -6 to 6
- blocks: int32 [3, 512], replicated, may hold values from 0 to 32767, as said below
Outputs:
- coefficients_out: float32 [32768, 1024], P('pts', 'out')
- residual_out: float32 [32768, 1024], P('pts', 'out')
Inputs may be any that keep to these rules, and one draw needn't show every extreme that they name: `blocks`: the 512 indices of a step are distinct.
All inputs are finite; a program needn't handle non-finite values.
Results may differ from a plain program's by a relative error of at most 0.0003.
Values may be sent and summed in bfloat16 or wider, within the bound.
No kernel may reach another device: no remote copies, remote signals or barrier semaphores. Data moves between devices by JAX's collectives and lax.ppermute only.
A program may use at most 128 MiB of HBM per device.

v0:
```python
import jax
import jax.numpy as jnp
from jax import lax
from jax.sharding import PartitionSpec as P

RIDGE = 0.5


def kernel(left_rows, right_rows, inverse_width):
    left_sq = jnp.sum(jnp.square(left_rows.astype(jnp.float32)), axis=1)
    right_sq = jnp.sum(jnp.square(right_rows.astype(jnp.float32)), axis=1)
    inner = lax.dot_general(
        left_rows, right_rows, (((1,), (1,)), ((), ())), preferred_element_type=jnp.float32
    )
    return jnp.exp(-inverse_width * (left_sq[:, None] + right_sq[None, :] - 2.0 * inner))


def local(points, coefficients, residual, blocks):
    local_count = points.shape[0]
    inverse_width = 1.0 / points.shape[1]
    position = lax.axis_index("pts")
    for number in range(blocks.shape[0]):
        chosen = blocks[number]
        offsets = chosen - position * local_count
        is_owned = (offsets >= 0) & (offsets < local_count)
        clipped = jnp.clip(offsets, 0, local_count - 1)
        owned_rows = jnp.where(is_owned[:, None], points[clipped].astype(jnp.float32), 0.0)
        owned_res = jnp.where(is_owned[:, None], residual[clipped], 0.0)
        summed = lax.psum(owned_rows.astype(jnp.bfloat16), "pts")
        block_res = lax.psum(owned_res, "pts")
        kernel_rows = kernel(points, summed, inverse_width)
        block_kernel = kernel(summed, summed, inverse_width)
        block_size = chosen.shape[0]
        factor = jnp.linalg.cholesky(block_kernel + RIDGE * jnp.eye(block_size, dtype=jnp.float32))
        update = jax.scipy.linalg.cho_solve((factor, True), block_res)
        product = jnp.dot(kernel_rows, update, precision=lax.Precision.HIGHEST)
        own_update = jnp.where(is_owned[:, None], update, 0.0)
        coefficients = coefficients.at[clipped].add(own_update)
        placed = jnp.zeros_like(residual).at[clipped].add(own_update)
        residual = residual - product - RIDGE * placed
    return (coefficients, residual)


def solution(mesh):
    return jax.shard_map(
        local,
        mesh=mesh,
        in_specs=(P("pts", None), P("pts", "out"), P("pts", "out"), P()),
        out_specs=(P("pts", "out"), P("pts", "out")),
        check_vma=False,
    )
```

profile of v0, /device:TPU:0, one launch (start us, length us, event | category | flops | bytes accessed | tf_op | source)
XLA Modules:
  0.0 701.5 jit_solution(9983994958240367674)
XLA Ops:
  46.6 62.1 %all-reduce.13.cloned.1.call-done = (bf16[512,1024]{1,0:T(8,128)(2,1)}, bf16[512,1024]{1,0:T(8,128)(2,1)}, bf16[512,1024]{1,0:T(8,128)(2,1)}) async-done(((bf16[512,1024]{1,0:T(8,128)(2,1)}, bf16[512,1024]{1,0:T(8,128)(2,1)}, bf16[512,1024]{1,0:T(8,128)(2,1)}), (bf16[512,1024]{1,0:T(8,128)(2,1)}, bf16[512,1024]{1,0:T(8,128)(2,1)}, bf16[512,1024]{1,0:T(8,128)(2,1)})) %all-reduce.13.cloned.1.call-update) | async-done | bytes 3145744 | tf_op jit(solution)/shard_map/psum | solution.py:29
  113.3 11.7 %cholesky.518 = f32[128,128]{1,0:T(8,128)S(1)} custom-call(f32[128,128]{1,0:T(8,128)S(1)} %cholesky.612), custom_call_target="Cholesky" | custom-call | tf_op jit(solution)/shard_map/jit(cholesky)/cholesky | solution.py:34
  125.0 9.8 %custom-call.41 = f32[1,128,128]{1,2,0:T(8,128)S(1)} custom-call(f32[1,128,128]{2,1,0:T(8,128)S(1)} %get-tuple-element.72), custom_call_target="InvertDiagBlocksLowerTriangular" | custom-call | tf_op jit(solution)/shard_map/jit(cholesky)/cholesky | solution.py:34
  135.7 12.1 %cholesky.537 = f32[128,128]{1,0:T(8,128)S(1)} custom-call(f32[128,128]{1,0:T(8,128)S(1)} %cholesky.616), custom_call_target="Cholesky" | custom-call | tf_op jit(solution)/shard_map/jit(cholesky)/cholesky | solution.py:34
  149.2 9.8 %custom-call.42 = f32[1,128,128]{1,2,0:T(8,128)S(1)} custom-call(f32[1,128,128]{2,1,0:T(8,128)S(1)} %get-tuple-element.69), custom_call_target="InvertDiagBlocksLowerTriangular" | custom-call | tf_op jit(solution)/shard_map/jit(cholesky)/cholesky | solution.py:34
  159.7 11.7 %cholesky.558 = f32[128,128]{1,0:T(8,128)S(1)} custom-call(f32[128,128]{1,0:T(8,128)S(1)} %cholesky.621), custom_call_target="Cholesky" | custom-call | tf_op jit(solution)/shard_map/jit(cholesky)/cholesky | solution.py:34
  172.0 9.8 %custom-call.43 = f32[1,128,128]{1,2,0:T(8,128)S(1)} custom-call(f32[1,128,128]{2,1,0:T(8,128)S(1)} %get-tuple-element.66), custom_call_target="InvertDiagBlocksLowerTriangular" | custom-call | tf_op jit(solution)/shard_map/jit(cholesky)/cholesky | solution.py:34
  182.4 11.9 %cholesky.575 = f32[128,128]{1,0:T(8,128)S(1)} custom-call(f32[128,128]{1,0:T(8,128)S(1)} %convolution_subtract_fusion.24), custom_call_target="Cholesky" | custom-call | tf_op jit(solution)/shard_map/jit(cholesky)/cholesky | solution.py:34
  212.4 11.7 %cholesky.446 = f32[128,128]{1,0:T(8,128)S(1)} custom-call(f32[128,128]{1,0:T(8,128)S(1)} %cholesky.599), custom_call_target="Cholesky" | custom-call | tf_op jit(solution)/shard_map/jit(cholesky)/cholesky | solution.py:34
  224.2 9.8 %custom-call.37 = f32[1,128,128]{1,2,0:T(8,128)S(1)} custom-call(f32[1,128,128]{2,1,0:T(8,128)S(1)} %get-tuple-element.82), custom_call_target="InvertDiagBlocksLowerTriangular" | custom-call | tf_op jit(solution)/shard_map/jit(cholesky)/cholesky | solution.py:34
  236.6 11.7 %cholesky.465 = f32[128,128]{1,0:T(8,128)S(1)} custom-call(f32[128,128]{1,0:T(8,128)S(1)} %cholesky.603), custom_call_target="Cholesky" | custom-call | tf_op jit(solution)/shard_map/jit(cholesky)/cholesky | solution.py:34
  249.7 10.2 %custom-call.38 = f32[1,128,128]{1,2,0:T(8,128)S(1)} custom-call(f32[1,128,128]{2,1,0:T(8,128)S(1)} %get-tuple-element.79), custom_call_target="InvertDiagBlocksLowerTriangular" | custom-call | tf_op jit(solution)/shard_map/jit(cholesky)/cholesky | solution.py:34
  261.5 11.7 %cholesky.486 = f32[128,128]{1,0:T(8,128)S(1)} custom-call(f32[128,128]{1,0:T(8,128)S(1)} %cholesky.608), custom_call_target="Cholesky" | custom-call | tf_op jit(solution)/shard_map/jit(cholesky)/cholesky | solution.py:34
  273.9 9.8 %custom-call.39 = f32[1,128,128]{1,2,0:T(8,128)S(1)} custom-call(f32[1,128,128]{2,1,0:T(8,128)S(1)} %get-tuple-element.76), custom_call_target="InvertDiagBlocksLowerTriangular" | custom-call | tf_op jit(solution)/shard_map/jit(cholesky)/cholesky | solution.py:34
  285.2 11.9 %cholesky.503 = f32[128,128]{1,0:T(8,128)S(1)} custom-call(f32[128,128]{1,0:T(8,128)S(1)} %convolution_subtract_fusion.25), custom_call_target="Cholesky" | custom-call | tf_op jit(solution)/shard_map/jit(cholesky)/cholesky | solution.py:34
  316.5 11.7 %cholesky.374 = f32[128,128]{1,0:T(8,128)S(1)} custom-call(f32[128,128]{1,0:T(8,128)S(1)} %cholesky.586), custom_call_target="Cholesky" | custom-call | tf_op jit(solution)/shard_map/jit(cholesky)/cholesky | solution.py:34
  328.2 9.8 %custom-call.33 = f32[1,128,128]{1,2,0:T(8,128)S(1)} custom-call(f32[1,128,128]{2,1,0:T(8,128)S(1)} %get-tuple-element.92), custom_call_target="InvertDiagBlocksLowerTriangular" | custom-call | tf_op jit(solution)/shard_map/jit(cholesky)/cholesky | solution.py:34
  340.7 11.7 %cholesky.393 = f32[128,128]{1,0:T(8,128)S(1)} custom-call(f32[128,128]{1,0:T(8,128)S(1)} %cholesky.590), custom_call_target="Cholesky" | custom-call | tf_op jit(solution)/shard_map/jit(cholesky)/cholesky | solution.py:34
  353.8 10.2 %custom-call.34 = f32[1,128,128]{1,2,0:T(8,128)S(1)} custom-call(f32[1,128,128]{2,1,0:T(8,128)S(1)} %get-tuple-element.89), custom_call_target="InvertDiagBlocksLowerTriangular" | custom-call | tf_op jit(solution)/shard_map/jit(cholesky)/cholesky | solution.py:34
  365.6 11.7 %cholesky.414 = f32[128,128]{1,0:T(8,128)S(1)} custom-call(f32[128,128]{1,0:T(8,128)S(1)} %cholesky.595), custom_call_target="Cholesky" | custom-call | tf_op jit(solution)/shard_map/jit(cholesky)/cholesky | solution.py:34
  378.0 9.8 %custom-call.35 = f32[1,128,128]{1,2,0:T(8,128)S(1)} custom-call(f32[1,128,128]{2,1,0:T(8,128)S(1)} %get-tuple-element.86), custom_call_target="InvertDiagBlocksLowerTriangular" | custom-call | tf_op jit(solution)/shard_map/jit(cholesky)/cholesky | solution.py:34
  389.3 11.9 %cholesky.431 = f32[128,128]{1,0:T(8,128)S(1)} custom-call(f32[128,128]{1,0:T(8,128)S(1)} %convolution_subtract_fusion.26), custom_call_target="Cholesky" | custom-call | tf_op jit(solution)/shard_map/jit(cholesky)/cholesky | solution.py:34
  405.5 11.9 %while.6 = (s32[]{:T(128)}, f32[512,512]{1,0:T(8,128)}, s32[4,2]{0,1:T(2,128)S(1)}, f32[4,128,128]{2,1,0:T(8,128)S(1)}, s32[]{:T(128)}) while((s32[]{:T(128)}, f32[512,512]{1,0:T(8,128)}, s32[4,2]{0,1:T(2,128)S(1)}, f32[4,128,128]{2,1,0:T(8,128)S(1)}, s32[]{:T(128)}) %tuple.99), condition=%wide.while_cond, body=%wide.while_body.sunk | while | flops 2 | bytes 131181 | solution.py:35
  417.4 11.5 %fusion.237 = f32[512,4096]{0,1:T(8,128)} fusion(bf16[512,1024]{1,0:T(8,128)(2,1)} %get-tuple-element.54, bf16[4096,1024]{1,0:T(8,128)(2,1)} %param.7), kind=kOutput, calls=%fused_computation.375 | convolution fusion | flops 4294967296 | bytes 17825792 | tf_op jit(solution)/shard_map/dot_general | solution.py:12
  428.9 39.3 %custom-call.36 = f32[4,128,128]{1,2,0:T(8,128)S(1)} custom-call(f32[4,128,128]{2,1,0:T(8,128)S(1)} %get-tuple-element.24), custom_call_target="InvertDiagBlocksLowerTriangular" | custom-call | tf_op jit(solution)/shard_map/jit(_cho_solve)/triangular_solve | solution.py:35
  485.5 12.8 %fusion.21 = f32[4096,256]{1,0:T(8,128)} fusion(f32[4096,256]{1,0:T(8,128)} %param.9, f32[512,4096]{0,1:T(8,128)} %fusion.237, f32[4096,256]{1,0:T(8,128)} %scatter_custom_fusion.1, f32[512]{0:T(512)S(1)} %multiply_reduce_fusion.3, f32[4096]{0:T(1024)S(1)} %multiply_reduce_fusion, f32[128,256]{1,0:T(8,128)S(1)} %fusion.197, f32[128,256]{1,0:T(8,128)S(1)} %fusion.195, ...), kind=kOutput, calls=%fused_computation.38 | convolution fusion | flops 6454378496 | bytes 21514240 | tf_op jit(solution)/shard_map/dot_general | solution.py:36
  504.7 11.5 %fusion.238 = f32[512,4096]{0,1:T(8,128)} fusion(bf16[512,1024]{1,0:T(8,128)(2,1)} %get-tuple-element.55, bf16[4096,1024]{1,0:T(8,128)(2,1)} %param.7), kind=kOutput, calls=%fused_computation.376 | convolution fusion | flops 4294967296 | bytes 17825792 | tf_op jit(solution)/shard_map/dot_general | solution.py:12
  516.2 40.5 %custom-call.40 = f32[4,128,128]{1,2,0:T(8,128)S(1)} custom-call(f32[4,128,128]{2,1,0:T(8,128)} %copy-done.3), custom_call_target="InvertDiagBlocksLowerTriangular" | custom-call | tf_op jit(solution)/shard_map/jit(_cho_solve)/triangular_solve | solution.py:35
  574.0 12.9 %fusion.27 = f32[4096,256]{1,0:T(8,128)} fusion(f32[4096,256]{1,0:T(8,128)} %fusion.21, f32[512,4096]{0,1:T(8,128)} %fusion.238, f32[4096,256]{1,0:T(8,128)} %scatter_custom_fusion.3, f32[512]{0:T(512)S(1)} %multiply_reduce_fusion.2, f32[4096]{0:T(1024)S(1)} %multiply_reduce_fusion, f32[128,256]{1,0:T(8,128)S(1)} %fusion.204, f32[128,256]{1,0:T(8,128)S(1)} %fusion.202, ...), kind=kOutput, calls=%fused_computation.40 | convolution fusion | flops 6454378496 | bytes 21514240 | tf_op jit(solution)/shard_map/dot_general | solution.py:36
  591.7 11.5 %fusion.239 = f32[512,4096]{0,1:T(8,128)} fusion(bf16[512,1024]{1,0:T(8,128)(2,1)} %get-tuple-element.56, bf16[4096,1024]{1,0:T(8,128)(2,1)} %param.7), kind=kOutput, calls=%fused_computation.377 | convolution fusion | flops 4294967296 | bytes 17825792 | tf_op jit(solution)/shard_map/dot_general | solution.py:12
  603.2 40.1 %custom-call.44 = f32[4,128,128]{1,2,0:T(8,128)S(1)} custom-call(f32[4,128,128]{2,1,0:T(8,128)} %copy-done.2), custom_call_target="InvertDiagBlocksLowerTriangular" | custom-call | tf_op jit(solution)/shard_map/jit(_cho_solve)/triangular_solve | solution.py:35
  673.5 13.0 %fusion.33 = f32[4096,256]{1,0:T(8,128)} fusion(f32[4096,256]{1,0:T(8,128)} %fusion.27, f32[512,4096]{0,1:T(8,128)} %fusion.239, f32[4096,256]{1,0:T(8,128)} %scatter_custom_fusion.5, f32[512]{0:T(512)S(1)} %multiply_reduce_fusion.1, f32[4096]{0:T(1024)S(1)} %multiply_reduce_fusion, f32[128,256]{1,0:T(8,128)S(1)} %fusion.211, f32[128,256]{1,0:T(8,128)S(1)} %fusion.209, ...), kind=kOutput, calls=%fused_computation.42 | convolution fusion | flops 6454378496 | bytes 21514240 | tf_op jit(solution)/shard_map/dot_general | solution.py:36
  (199 shorter events, 209.3 us)
Async XLA Ops:
  7.2 4.5 copy-start.4
  7.2 101.5 %all-reduce.13.cloned.1.call-start = ((), (), s32[]{:S(2)}) async-start(), calls=%async_computation.3 | async-start | bytes 6291456 | tf_op jit(solution)/shard_map/psum | solution.py:29
  36.4 431.9 %all-reduce.7.cloned.1.call-start = ((), (), s32[]{:S(2)}) async-start(), calls=%async_computation | async-start | bytes 1048576 | tf_op jit(solution)/shard_map/psum | solution.py:30
  41.1 518.7 %all-reduce.9.cloned.1.call-start = ((), (), s32[]{:S(2)}) async-start(), calls=%async_computation.1 | async-start | bytes 1048576 | tf_op jit(solution)/shard_map/psum | solution.py:30
  206.1 0.7 copy-start.2
  211.4 1.0 copy-start
  308.8 6.7 copy-start.3
  315.5 1.0 copy-start.1
  504.7 154.8 %all-reduce.11.cloned.1.call-start = ((), (), s32[]{:S(2)}) async-start(), calls=%async_computation.2 | async-start | bytes 1048576 | tf_op jit(solution)/shard_map/psum | solution.py:30
Sparse Core Ops, SparseCore 0:
  36.5 72.1 all-reduce.12
  111.8 55.1 all-reduce.6
  504.8 55.0 all-reduce.8
  591.8 54.6 all-reduce.10
where the time goes:
time: 710 us; the launch traced here: 701 us
  other arithmetic  421 us (59%)
  matrix products  120 us (17%)
  local copies, waits for them, and re-layouts  71.3 us (10%)
  waiting for transfers between devices  65.4 us (9%)
  between operations  22.8 us (3%)
    another operation x45, other arithmetic, local(): jnp.linalg.cholesky(block_kernel + RIDGE * jnp.eye(block_size, dtype=jnp....  239 us
    another operation x7, other arithmetic, local(): update = jax.scipy.linalg.cho_solve((factor, True), block_res)  121 us
    psum x1, waiting for transfers between devices, local(): summed = lax.psum(owned_rows.astype(jnp.bfloat16), 'pts')  62.1 us
    dot_general x6, matrix products, kernel(): lax.dot_general(left_rows, right_rows, (((1,), (1,)), ((), ())), preferre...  42 us
    dot_general x3, matrix products, local(): product = jnp.dot(kernel_rows, update, precision=lax.Precision.HIGHEST)  38.7 us
    another operation x40, local copies, waits for them, and re-layouts, local(): update = jax.scipy.linalg.cho_solve((factor, True), block_res)  28.3 us
    another operation x42, matrix products, local(): update = jax.scipy.linalg.cho_solve((factor, True), block_res)  26.9 us
    scatter-add x3, other arithmetic, local(): coefficients = coefficients.at[clipped].add(own_update)  24 us
  transfers between devices with their start and end apart: 4, of which 2 were waited for; matrix products, arithmetic and copies ran while one was open for 68% of the time, Pallas kernels for 0%

commit v1 on v0

--- a/solution.py
+++ b/solution.py
@@ -26,7 +26,7 @@
         clipped = jnp.clip(offsets, 0, local_count - 1)
         owned_rows = jnp.where(is_owned[:, None], points[clipped].astype(jnp.float32), 0.0)
         owned_res = jnp.where(is_owned[:, None], residual[clipped], 0.0)
-        summed = lax.psum(owned_rows.astype(jnp.bfloat16), "pts")
+        summed = jnp.sum(lax.all_gather(owned_rows.astype(jnp.bfloat16), "pts"), axis=0)
         block_res = lax.psum(owned_res, "pts")
         kernel_rows = kernel(points, summed, inverse_width)
         block_kernel = kernel(summed, summed, inverse_width)

time: 710 us -> 832 us (1.17)
  waiting for transfers between devices: 65.4 us -> 158 us
  matrix products: 120 us -> 136 us
  other arithmetic: 421 us -> 434 us
    all_gather x0 -> x3, waiting for transfers between devices: none -> 108 us  [local(): lax.all_gather(owned_rows.astype(jnp.bfloat16), 'pts')]
    psum x1 -> x0, waiting for transfers between devices: 62.1 us -> none  [local(): summed = lax.psum(owned_rows.astype(jnp.bfloat16), 'pts')]
    psum x3, waiting for transfers between devices: 3.15 us -> 50.2 us  [local(): block_res = lax.psum(owned_res, 'pts')]
    dot_general x3, matrix products: 38.7 us -> 57.2 us  [local(): product = jnp.dot(kernel_rows, update, precision=lax.Precision.HIGHEST)]
    reduce_sum x0 -> x3, other arithmetic: none -> 17 us  [local(): jnp.sum(lax.all_gather(owned_rows.astype(jnp.bfloat16), 'pts'), axis=0)]
    another operation x45 -> x42, other arithmetic: 239 us -> 239 us  [local(): jnp.linalg.cholesky(block_kernel + RIDGE * jnp.eye(block_size, dtype=jnp....]
  transfers between devices with their start and end apart: 4 -> 6, of which waited for: 2 -> 4; matrix products, arithmetic and copies ran while one was open for 68% -> 61% of each run, Pallas kernels for 0% -> 0%
where the time goes in v1:
time: 832 us; the launch traced here: 824 us
  other arithmetic  434 us (52%)
  waiting for transfers between devices  158 us (19%)
  matrix products  136 us (16%)
  local copies, waits for them, and re-layouts  71.5 us (9%)
  between operations  22.7 us (3%)
    another operation x42, other arithmetic, local(): jnp.linalg.cholesky(block_kernel + RIDGE * jnp.eye(block_size, dtype=jnp....  239 us
    another operation x7, other arithmetic, local(): update = jax.scipy.linalg.cho_solve((factor, True), block_res)  121 us
    all_gather x3, waiting for transfers between devices, local(): lax.all_gather(owned_rows.astype(jnp.bfloat16), 'pts')  108 us
    dot_general x3, matrix products, local(): product = jnp.dot(kernel_rows, update, precision=lax.Precision.HIGHEST)  57.2 us
    psum x3, waiting for transfers between devices, local(): block_res = lax.psum(owned_res, 'pts')  50.2 us
    dot_general x6, matrix products, kernel(): lax.dot_general(left_rows, right_rows, (((1,), (1,)), ((), ())), preferre...  35.6 us
    another operation x40, local copies, waits for them, and re-layouts, local(): update = jax.scipy.linalg.cho_solve((factor, True), block_res)  27.8 us
    another operation x42, matrix products, local(): update = jax.scipy.linalg.cho_solve((factor, True), block_res)  26.9 us
  transfers between devices with their start and end apart: 6, of which 4 were waited for; matrix products, arithmetic and copies ran while one was open for 61% of the time, Pallas kernels for 0%

profile of v1, /device:TPU:0, one launch (start us, length us, event | category | flops | bytes accessed | tf_op | source)
XLA Modules:
  0.0 823.8 jit_solution(9572671621633139903)
XLA Ops:
  48.6 28.8 %all-gather.4.cloned.1.call-done = bf16[8,512,1024]{2,1,0:T(8,128)(2,1)} async-done(((bf16[1,512,1024]{2,1,0:T(8,128)(2,1)}), bf16[8,512,1024]{2,1,0:T(8,128)(2,1)}) %all-gather.4.cloned.1.call-update) | async-done | bytes 8388624 | tf_op jit(solution)/shard_map/all_gather | solution.py:29
  83.3 10.6 %fusion.240 = f32[512,4096]{1,0:T(8,128)} fusion(bf16[512,1024]{1,0:T(8,128)(2,1)S(1)} %reduce_sum.77, bf16[4096,1024]{1,0:T(8,128)(2,1)} %param.7), kind=kOutput, calls=%fused_computation.378 | convolution fusion | flops 4294967296 | bytes 17825792 | tf_op jit(solution)/shard_map/dot_general | solution.py:12
  93.9 39.6 %all-gather.6.cloned.1.call-done = bf16[8,512,1024]{2,1,0:T(8,128)(2,1)} async-done(((bf16[1,512,1024]{2,1,0:T(8,128)(2,1)}), bf16[8,512,1024]{2,1,0:T(8,128)(2,1)}) %all-gather.6.cloned.1.call-update) | async-done | bytes 8388624 | tf_op jit(solution)/shard_map/all_gather | solution.py:29
  139.5 10.5 %fusion.241 = f32[512,4096]{1,0:T(8,128)} fusion(bf16[512,1024]{1,0:T(8,128)(2,1)S(1)} %reduce_sum.79, bf16[4096,1024]{1,0:T(8,128)(2,1)} %param.7), kind=kOutput, calls=%fused_computation.379 | convolution fusion | flops 4294967296 | bytes 17825792 | tf_op jit(solution)/shard_map/dot_general | solution.py:12
  150.0 39.7 %all-gather.8.cloned.1.call-done = bf16[8,512,1024]{2,1,0:T(8,128)(2,1)} async-done(((bf16[1,512,1024]{2,1,0:T(8,128)(2,1)}), bf16[8,512,1024]{2,1,0:T(8,128)(2,1)}) %all-gather.8.cloned.1.call-update) | async-done | bytes 8388624 | tf_op jit(solution)/shard_map/all_gather | solution.py:29
  195.7 10.4 %fusion.242 = f32[512,4096]{1,0:T(8,128)} fusion(bf16[512,1024]{1,0:T(8,128)(2,1)S(1)} %reduce_sum.85, bf16[4096,1024]{1,0:T(8,128)(2,1)} %param.7), kind=kOutput, calls=%fused_computation.380 | convolution fusion | flops 4294967296 | bytes 17825792 | tf_op jit(solution)/shard_map/dot_general | solution.py:12
  208.5 11.7 %cholesky.518 = f32[128,128]{1,0:T(8,128)S(1)} custom-call(f32[128,128]{1,0:T(8,128)S(1)} %cholesky.612), custom_call_target="Cholesky" | custom-call | tf_op jit(solution)/shard_map/jit(cholesky)/cholesky | solution.py:34
  220.3 9.8 %custom-call.41 = f32[1,128,128]{1,2,0:T(8,128)S(1)} custom-call(f32[1,128,128]{2,1,0:T(8,128)S(1)} %get-tuple-element.69), custom_call_target="InvertDiagBlocksLowerTriangular" | custom-call | tf_op jit(solution)/shard_map/jit(cholesky)/cholesky | solution.py:34
  232.7 11.7 %cholesky.537 = f32[128,128]{1,0:T(8,128)S(1)} custom-call(f32[128,128]{1,0:T(8,128)S(1)} %cholesky.616), custom_call_target="Cholesky" | custom-call | tf_op jit(solution)/shard_map/jit(cholesky)/cholesky | solution.py:34
  244.5 10.0 %custom-call.42 = f32[1,128,128]{1,2,0:T(8,128)S(1)} custom-call(f32[1,128,128]{2,1,0:T(8,128)S(1)} %get-tuple-element.66), custom_call_target="InvertDiagBlocksLowerTriangular" | custom-call | tf_op jit(solution)/shard_map/jit(cholesky)/cholesky | solution.py:34
  256.1 11.7 %cholesky.558 = f32[128,128]{1,0:T(8,128)S(1)} custom-call(f32[128,128]{1,0:T(8,128)S(1)} %cholesky.621), custom_call_target="Cholesky" | custom-call | tf_op jit(solution)/shard_map/jit(cholesky)/cholesky | solution.py:34
  279.6 12.7 %cholesky.575 = f32[128,128]{1,0:T(8,128)} custom-call(f32[128,128]{1,0:T(8,128)S(1)} %convolution_subtract_fusion.24), custom_call_target="Cholesky" | custom-call | tf_op jit(solution)/shard_map/jit(cholesky)/cholesky | solution.py:34
  294.8 11.7 %cholesky.446 = f32[128,128]{1,0:T(8,128)S(1)} custom-call(f32[128,128]{1,0:T(8,128)S(1)} %cholesky.599), custom_call_target="Cholesky" | custom-call | tf_op jit(solution)/shard_map/jit(cholesky)/cholesky | solution.py:34
  306.5 9.8 %custom-call.37 = f32[1,128,128]{1,2,0:T(8,128)S(1)} custom-call(f32[1,128,128]{2,1,0:T(8,128)S(1)} %get-tuple-element.79), custom_call_target="InvertDiagBlocksLowerTriangular" | custom-call | tf_op jit(solution)/shard_map/jit(cholesky)/cholesky | solution.py:34
  319.0 11.7 %cholesky.465 = f32[128,128]{1,0:T(8,128)S(1)} custom-call(f32[128,128]{1,0:T(8,128)S(1)} %cholesky.603), custom_call_target="Cholesky" | custom-call | tf_op jit(solution)/shard_map/jit(cholesky)/cholesky | solution.py:34
  330.9 9.8 %custom-call.38 = f32[1,128,128]{1,2,0:T(8,128)S(1)} custom-call(f32[1,128,128]{2,1,0:T(8,128)S(1)} %get-tuple-element.76), custom_call_target="InvertDiagBlocksLowerTriangular" | custom-call | tf_op jit(solution)/shard_map/jit(cholesky)/cholesky | solution.py:34
  342.3 11.7 %cholesky.486 = f32[128,128]{1,0:T(8,128)S(1)} custom-call(f32[128,128]{1,0:T(8,128)S(1)} %cholesky.608), custom_call_target="Cholesky" | custom-call | tf_op jit(solution)/shard_map/jit(cholesky)/cholesky | solution.py:34
  366.0 12.1 %cholesky.503 = f32[128,128]{1,0:T(8,128)S(1)} custom-call(f32[128,128]{1,0:T(8,128)S(1)} %convolution_subtract_fusion.25), custom_call_target="Cholesky" | custom-call | tf_op jit(solution)/shard_map/jit(cholesky)/cholesky | solution.py:34
  396.9 11.7 %cholesky.374 = f32[128,128]{1,0:T(8,128)S(1)} custom-call(f32[128,128]{1,0:T(8,128)S(1)} %cholesky.586), custom_call_target="Cholesky" | custom-call | tf_op jit(solution)/shard_map/jit(cholesky)/cholesky | solution.py:34
  408.6 9.8 %custom-call.33 = f32[1,128,128]{1,2,0:T(8,128)S(1)} custom-call(f32[1,128,128]{2,1,0:T(8,128)S(1)} %get-tuple-element.89), custom_call_target="InvertDiagBlocksLowerTriangular" | custom-call | tf_op jit(solution)/shard_map/jit(cholesky)/cholesky | solution.py:34
  421.1 11.7 %cholesky.393 = f32[128,128]{1,0:T(8,128)S(1)} custom-call(f32[128,128]{1,0:T(8,128)S(1)} %cholesky.590), custom_call_target="Cholesky" | custom-call | tf_op jit(solution)/shard_map/jit(cholesky)/cholesky | solution.py:34
  432.8 9.9 %custom-call.34 = f32[1,128,128]{1,2,0:T(8,128)S(1)} custom-call(f32[1,128,128]{2,1,0:T(8,128)S(1)} %get-tuple-element.86), custom_call_target="InvertDiagBlocksLowerTriangular" | custom-call | tf_op jit(solution)/shard_map/jit(cholesky)/cholesky | solution.py:34
  444.4 11.7 %cholesky.414 = f32[128,128]{1,0:T(8,128)S(1)} custom-call(f32[128,128]{1,0:T(8,128)S(1)} %cholesky.595), custom_call_target="Cholesky" | custom-call | tf_op jit(solution)/shard_map/jit(cholesky)/cholesky | solution.py:34
  468.0 11.9 %cholesky.431 = f32[128,128]{1,0:T(8,128)S(1)} custom-call(f32[128,128]{1,0:T(8,128)S(1)} %convolution_subtract_fusion.26), custom_call_target="Cholesky" | custom-call | tf_op jit(solution)/shard_map/jit(cholesky)/cholesky | solution.py:34
  484.8 11.3 %while.6 = (s32[]{:T(128)}, f32[512,512]{1,0:T(8,128)}, s32[4,2]{0,1:T(2,128)S(1)}, f32[4,128,128]{2,1,0:T(8,128)S(1)}, s32[]{:T(128)}) while((s32[]{:T(128)}, f32[512,512]{1,0:T(8,128)}, s32[4,2]{0,1:T(2,128)S(1)}, f32[4,128,128]{2,1,0:T(8,128)S(1)}, s32[]{:T(128)}) %tuple.104), condition=%wide.while_cond, body=%wide.while_body.sunk | while | flops 2 | bytes 131181 | solution.py:35
  496.1 40.1 %custom-call.40 = f32[4,128,128]{1,2,0:T(8,128)S(1)} custom-call(f32[4,128,128]{2,1,0:T(8,128)} %copy-done.5), custom_call_target="InvertDiagBlocksLowerTriangular" | custom-call | tf_op jit(solution)/shard_map/jit(_cho_solve)/triangular_solve | solution.py:35
  536.2 39.3 %custom-call.36 = f32[4,128,128]{1,2,0:T(8,128)S(1)} custom-call(f32[4,128,128]{2,1,0:T(8,128)S(1)} %get-tuple-element.24), custom_call_target="InvertDiagBlocksLowerTriangular" | custom-call | tf_op jit(solution)/shard_map/jit(_cho_solve)/triangular_solve | solution.py:35
  594.9 19.0 %fusion.21 = f32[4096,256]{1,0:T(8,128)} fusion(f32[4096,256]{1,0:T(8,128)} %param.9, f32[512,4096]{1,0:T(8,128)} %fusion.240, f32[4096,256]{1,0:T(8,128)} %scatter_custom_fusion.1, f32[512]{0:T(512)S(1)} %multiply_reduce_fusion.3, f32[4096]{0:T(1024)S(1)} %multiply_reduce_fusion, f32[128,256]{1,0:T(8,128)S(1)} %fusion.200, f32[128,256]{1,0:T(8,128)S(1)} %fusion.198, ...), kind=kOutput, calls=%fused_computation.38 | convolution fusion | flops 6454378496 | bytes 21514240 | tf_op jit(solution)/shard_map/dot_general | solution.py:36
  623.2 50.2 %all-reduce.7.cloned.1.call-done = f32[512,256]{1,0:T(8,128)} async-done(((f32[512,256]{1,0:T(8,128)}), f32[512,256]{1,0:T(8,128)}) %all-reduce.7.cloned.1.call-update) | async-done | bytes 524304 | tf_op jit(solution)/shard_map/psum | solution.py:30
  687.7 19.0 %fusion.27 = f32[4096,256]{1,0:T(8,128)} fusion(f32[4096,256]{1,0:T(8,128)} %fusion.21, f32[512,4096]{1,0:T(8,128)} %fusion.241, f32[4096,256]{1,0:T(8,128)} %scatter_custom_fusion.3, f32[512]{0:T(512)S(1)} %multiply_reduce_fusion.2, f32[4096]{0:T(1024)S(1)} %multiply_reduce_fusion, f32[128,256]{1,0:T(8,128)S(1)} %fusion.207, f32[128,256]{1,0:T(8,128)S(1)} %fusion.205, ...), kind=kOutput, calls=%fused_computation.40 | convolution fusion | flops 6454378496 | bytes 21514240 | tf_op jit(solution)/shard_map/dot_general | solution.py:36
  720.0 39.3 %custom-call.44 = f32[4,128,128]{1,2,0:T(8,128)S(1)} custom-call(f32[4,128,128]{2,1,0:T(8,128)S(1)} %get-tuple-element.26), custom_call_target="InvertDiagBlocksLowerTriangular" | custom-call | tf_op jit(solution)/shard_map/jit(_cho_solve)/triangular_solve | solution.py:35
  789.7 19.2 %fusion.33 = f32[4096,256]{1,0:T(8,128)} fusion(f32[4096,256]{1,0:T(8,128)} %fusion.27, f32[512,4096]{1,0:T(8,128)} %fusion.242, f32[4096,256]{1,0:T(8,128)} %scatter_custom_fusion.5, f32[512]{0:T(512)S(1)} %multiply_reduce_fusion.1, f32[4096]{0:T(1024)S(1)} %multiply_reduce_fusion, f32[128,256]{1,0:T(8,128)S(1)} %fusion.214, f32[128,256]{1,0:T(8,128)S(1)} %fusion.212, ...), kind=kOutput, calls=%fused_computation.42 | convolution fusion | flops 6454378496 | bytes 21514240 | tf_op jit(solution)/shard_map/dot_general | solution.py:36
  (212 shorter events, 250.6 us)
Async XLA Ops:
  7.2 4.5 copy-start.7
  7.2 70.2 %all-gather.4.cloned.1.call-start = ((), (), s32[]{:S(2)}) async-start(), calls=%async_computation | async-start | bytes 9437184 | tf_op jit(solution)/shard_map/all_gather | solution.py:29
  20.2 113.3 %all-gather.6.cloned.1.call-start = ((), (), s32[]{:S(2)}) async-start(), calls=%async_computation.2 | async-start | bytes 9437184 | tf_op jit(solution)/shard_map/all_gather | solution.py:29
  28.7 161.0 %all-gather.8.cloned.1.call-start = ((), (), s32[]{:S(2)}) async-start(), calls=%async_computation.4 | async-start | bytes 9437184 | tf_op jit(solution)/shard_map/all_gather | solution.py:29
  38.2 539.4 %all-reduce.5.cloned.1.call-start = ((), (), s32[]{:S(2)}) async-start(), calls=%async_computation.1 | async-start | bytes 1048576 | tf_op jit(solution)/shard_map/psum | solution.py:30
  43.0 630.5 %all-reduce.7.cloned.1.call-start = ((), (), s32[]{:S(2)}) async-start(), calls=%async_computation.3 | async-start | bytes 1048576 | tf_op jit(solution)/shard_map/psum | solution.py:30
  83.0 10.9 %copy-start.1 = (bf16[512,1024]{1,0:T(8,128)(2,1)}, bf16[512,1024]{1,0:T(8,128)(2,1)S(1)}, u32[]{:S(2)}) copy-start(bf16[512,1024]{1,0:T(8,128)(2,1)S(1)} %reduce_sum.77) | copy-start | bytes 3145732
  207.4 1.1 copy-start.4
  293.7 1.1 copy-start.2
  390.6 5.2 copy-start.5
  395.9 1.0 copy-start.3
  442.8 53.3 %copy-start.6 = (f32[128,128]{1,0:T(8,128)S(1)}, f32[128,128]{1,0:T(8,128)}, u32[]{:S(2)}) copy-start(f32[128,128]{1,0:T(8,128)} %cholesky.575) | copy-start | bytes 196612
  618.7 156.9 %all-reduce.9.cloned.1.call-start = ((), (), s32[]{:S(2)}) async-start(), calls=%async_computation.5 | async-start | bytes 1048576 | tf_op jit(solution)/shard_map/psum | solution.py:30
  706.7 4.9 copy-start
Sparse Core Ops, SparseCore 0:
  20.3 56.9 all-gather.3
  79.2 54.2 all-gather.5
  135.4 54.2 all-gather.7
  192.7 55.3 all-reduce.4
  618.8 54.6 all-reduce.6
  711.7 54.4 all-reduce.8
